TPU v7x, 128 devices: a whole 4x4x4 slice. The times are simulated.
128 devices in a mesh: seq: 32 (over x, y, core), head: 4 (over z).
Axes of the slice: x: 4, y: 4, z: 4, core: 2. Of those that a mesh axis runs over, the one named last changes fastest.
Arguments:
- vis_tokens: bfloat16 [12288, 1408], P('seq'), may hold values from -70 to 70
- vis_counts: int32 [4, 8], replicated, may hold values from 1 to 384, 1536 in all within a row
- vis_spatial: int32 [4, 96], replicated, may hold values from 0 to 1023, as said below
- enc_gain: float32 [1408], replicated, may hold values from 0.25 to 1.75
- enc_bias: float32 [1408], replicated, may hold values from -3 to 3
- enc_qkv: bfloat16 [3, 1408, 1408], P(None, None, 'head'), may hold values from -6 to 6
- enc_proj: bfloat16 [1408, 1408], P('head'), may hold values from -0.15625 to 0.15625
- final_gain: float32 [1408], replicated, may hold values from 0.25 to 1.75
- final_bias: float32 [1408], replicated, may hold values from -3 to 3
- to_decoder: bfloat16 [1408, 512], replicated, may hold values from -0.15625 to 0.15625
- mask_token: float32 [512], replicated, may hold values from -4 to 4
- dec_gain: float32 [512], replicated, may hold values from 0.25 to 1.75
- dec_bias: float32 [512], replicated, may hold values from -3 to 3
- dec_qkv: bfloat16 [3, 512, 512], P(None, None, 'head'), may hold values from -11 to 11
Outputs:
- decoded: bfloat16 [4, 16, 1024, 512], P(None, None, 'seq', 'head')
Inputs may be any that keep to these rules, and one draw needn't show every extreme that they name: `vis_spatial`: row c lists in increasing order the spatial positions visible in every frame of clip c; each aligned run of 32 spatial positions holds exactly 3 of them. The visible tokens of clip c, in order of position, lie on the members of its encoder group in order, vis_counts[c, g] of them on member g; each row sums to 1536.
All inputs are finite; a program needn't handle non-finite values.
Results may differ from a plain program's by a relative error of at most 0.015.
Values may be sent and summed in bfloat16 or wider, within the bound.
A program may use at most 320 MiB of HBM per device.

v0:
```python
import math
import jax
import jax.numpy as jnp
from jax import lax
from jax.sharding import PartitionSpec as P

D = 1408
HEADS = 16
DD = 512
DHEADS = 8
S = 1024
BLOCK = 32
GROUP = 8
L = 16384
VSP = 96
VIS = 1536
epsilon = 1e-06
floor_score = -1e30


def from_partner(block, axis, distance):
    count = lax.axis_size(axis)
    route = []
    for low in range(count):
        high = low | 1 << distance
        if high != low and high < count:
            route += [(low, high), (high, low)]
    return lax.ppermute(block, axis, route)


def layer_norm(values, gain_row, bias_row):
    centre = jnp.mean(values, axis=-1, keepdims=True)
    centred = values - centre
    spread = jnp.mean(centred * centred, axis=-1, keepdims=True)
    return centred * lax.rsqrt(spread + epsilon) * gain_row + bias_row


def sinusoid(positions, table_width):
    column_ids = jnp.arange(table_width, dtype=jnp.int32)
    exponent = (2 * (column_ids // 2)).astype(jnp.float32) / table_width
    frequency = jnp.exp(exponent * -math.log(10000.0))
    angles = positions.astype(jnp.float32)[:, None] * frequency[None, :]
    return jnp.where(column_ids[None, :] % 2 == 0, jnp.sin(angles), jnp.cos(angles))


def fold_block(fold_state, queries, key_rows, value_rows, allowed, score_scale):
    running_max, running_sum, running_acc = fold_state
    scores = jnp.einsum("cqhe,ckhe->chqk", queries, key_rows, preferred_element_type=jnp.float32)
    allowed_grid = allowed[:, None, None, :]
    scores = jnp.where(allowed_grid, scores * score_scale, floor_score)
    new_max = jnp.maximum(running_max, jnp.max(scores, axis=-1))
    factor = jnp.exp(running_max - new_max)
    raised = jnp.where(allowed_grid, jnp.exp(scores - new_max[..., None]), 0.0)
    running_sum = running_sum * factor + jnp.sum(raised, axis=-1)
    weights = raised.astype(jnp.bfloat16)
    update = jnp.einsum("chqk,ckhe->chqe", weights, value_rows, preferred_element_type=jnp.float32)
    running_acc = running_acc * factor[..., None] + update
    return (new_max, running_sum, running_acc)


def empty_state(batch_count, head_count, query_count, head_size):
    return (
        jnp.full((batch_count, head_count, query_count), floor_score, jnp.float32),
        jnp.zeros((batch_count, head_count, query_count), jnp.float32),
        jnp.zeros((batch_count, head_count, query_count, head_size), jnp.float32),
    )


def body(
    vis_tokens,
    vis_counts,
    vis_spatial,
    enc_gain,
    enc_bias,
    enc_qkv,
    enc_proj,
    final_gain,
    final_bias,
    to_decoder,
    mask_token,
    dec_gain,
    dec_bias,
    dec_qkv,
):
    seq_count = lax.axis_size("seq")
    seq_index = lax.axis_index("seq")
    clips = vis_counts.shape[0]
    clip_index = seq_index % clips
    member = seq_index // clips
    slot_count = vis_tokens.shape[0]
    slot_ids = jnp.arange(slot_count, dtype=jnp.int32)
    member_ids = jnp.arange(GROUP, dtype=jnp.int32)
    group_counts = lax.dynamic_index_in_dim(vis_counts, clip_index, 0, keepdims=False)
    before = jnp.sum(jnp.where(member_ids < member, group_counts, 0))
    slot_live = slot_ids < jnp.sum(jnp.where(member_ids == member, group_counts, 0))
    token_rows = vis_tokens.astype(jnp.float32)
    normed = layer_norm(token_rows, enc_gain, enc_bias).astype(jnp.bfloat16)
    enc_parts = [
        jnp.dot(normed, enc_qkv[part_id], preferred_element_type=jnp.float32).astype(jnp.bfloat16)
        for part_id in range(3)
    ]
    head_size = D // HEADS
    enc_width = enc_parts[0].shape[1]
    local_heads = enc_width // head_size
    enc_queries = enc_parts[0].reshape(1, slot_count, local_heads, head_size)
    key_value = jnp.stack([enc_parts[1], enc_parts[2]])
    enc_scale = 1.0 / math.sqrt(head_size)
    clip_bits = clips.bit_length() - 1
    collected = key_value[None]
    for bit in range(GROUP.bit_length() - 1):
        partner = from_partner(collected, "seq", bit + clip_bits)
        upper_side = (member >> bit) % 2 == 1
        collected = jnp.where(
            upper_side,
            jnp.concatenate([partner, collected], axis=0),
            jnp.concatenate([collected, partner], axis=0),
        )
    group_keys = jnp.moveaxis(collected, 1, 0).reshape(
        2, 1, GROUP * slot_count, local_heads, head_size
    )
    group_live = (slot_ids[None, :] < group_counts[:, None]).reshape(1, GROUP * slot_count)
    fold_state = fold_block(
        empty_state(1, local_heads, slot_count, head_size),
        enc_queries,
        group_keys[0],
        group_keys[1],
        group_live,
        enc_scale,
    )
    context = fold_state[2][0] / fold_state[1][0][..., None]
    context = jnp.transpose(context, (1, 0, 2)).reshape(slot_count, enc_width).astype(jnp.bfloat16)
    partial_out = jnp.dot(context, enc_proj, preferred_element_type=jnp.float32)
    attended = lax.psum(partial_out.astype(jnp.bfloat16), "head").astype(jnp.float32)
    residual = token_rows + attended
    final_rows = layer_norm(residual, final_gain, final_bias).astype(jnp.bfloat16)
    encoded = jnp.dot(final_rows, to_decoder, preferred_element_type=jnp.float32).astype(
        jnp.bfloat16
    )
    visible_index = jnp.minimum(before + slot_ids, VIS - 1)
    spatial_row = lax.dynamic_index_in_dim(vis_spatial, clip_index, 0, keepdims=False)
    spatial_ids = jnp.arange(VSP, dtype=jnp.int32)
    spatial = jnp.sum(
        jnp.where((visible_index % VSP)[:, None] == spatial_ids[None, :], spatial_row[None, :], 0),
        axis=1,
    )
    position = visible_index // VSP * S + spatial
    block_index = position // BLOCK
    owner_index = block_index % seq_count
    own_rows = L // seq_count
    local_row = clip_index * own_rows + block_index // seq_count * BLOCK + position % BLOCK
    per_peer = slot_count // seq_count
    peer_ids = jnp.arange(seq_count, dtype=jnp.int32)
    owner_hits = ((owner_index[:, None] == peer_ids[None, :]) & slot_live[:, None]).astype(
        jnp.float32
    )
    earlier_mask = (slot_ids[None, :] < slot_ids[:, None]).astype(jnp.float32)
    earlier = jnp.dot(earlier_mask, owner_hits, precision=lax.Precision.HIGHEST)
    bucket_rank = jnp.sum(earlier * owner_hits, axis=1).astype(jnp.int32)
    target = jnp.where(slot_live, owner_index * per_peer + bucket_rank, -1)
    bucket_ids = jnp.arange(seq_count * per_peer, dtype=jnp.int32)
    chosen = target[None, :] == bucket_ids[:, None]
    send_rows = (
        jnp.dot(chosen.astype(jnp.bfloat16), encoded, preferred_element_type=jnp.float32)
        .astype(jnp.bfloat16)
        .reshape(seq_count, per_peer, DD)
    )
    send_index = jnp.max(jnp.where(chosen, local_row[None, :], -1), axis=1).reshape(
        seq_count, per_peer
    )
    got_rows, got_index = (
        lax.all_to_all(send_rows, "seq", split_axis=0, concat_axis=0, tiled=True),
        lax.all_to_all(send_index, "seq", split_axis=0, concat_axis=0, tiled=True),
    )
    total_rows = clips * own_rows
    got_index = jnp.where(got_index < 0, total_rows, got_index).reshape(-1)
    placed = (
        jnp.zeros((total_rows, DD), jnp.float32)
        .at[got_index]
        .set(got_rows.reshape(-1, DD).astype(jnp.float32), mode="drop")
    )
    row_ids = jnp.arange(own_rows, dtype=jnp.int32)
    local_position = (row_ids // BLOCK * seq_count + seq_index) * BLOCK + row_ids % BLOCK
    frame_ids = jnp.arange(S, dtype=jnp.int32)
    spatial_flags = jnp.any(vis_spatial[:, :, None] == frame_ids[None, None, :], axis=1)
    column_pick = ((local_position % S)[:, None] == frame_ids[None, :]).astype(jnp.float32)
    seen_flags = (
        jnp.einsum(
            "cs,rs->cr",
            spatial_flags.astype(jnp.float32),
            column_pick,
            precision=lax.Precision.HIGHEST,
        )
        > 0.5
    )
    inputs = sinusoid(local_position, DD)[None] + jnp.where(
        seen_flags[..., None], placed.reshape(clips, own_rows, DD), mask_token[None, None, :]
    )
    dec_normed = layer_norm(inputs, dec_gain, dec_bias).astype(jnp.bfloat16)
    dec_size = DD // DHEADS
    dec_query = jnp.einsum(
        "crd,de->cre", dec_normed, dec_qkv[0], preferred_element_type=jnp.float32
    ).astype(jnp.bfloat16)
    dec_width = dec_query.shape[2]
    dec_heads = dec_width // dec_size
    dec_queries = dec_query.reshape(clips, own_rows, dec_heads, dec_size)
    dec_scale = 1.0 / math.sqrt(dec_size)
    start_state = empty_state(clips, dec_heads, own_rows, dec_size)
    dec_key = jnp.einsum(
        "crd,de->cre", dec_normed, dec_qkv[1], preferred_element_type=jnp.float32
    ).astype(jnp.bfloat16)
    dec_value = jnp.einsum(
        "crd,de->cre", dec_normed, dec_qkv[2], preferred_element_type=jnp.float32
    ).astype(jnp.bfloat16)
    stacked = jnp.stack([dec_key, dec_value])
    shard_part = lax.all_gather(stacked, "seq", axis=2, tiled=True)
    row_count = shard_part.shape[2]
    block_count = row_count // own_rows
    block_rows = row_count // block_count
    grouped = jnp.moveaxis(
        shard_part.reshape(2, clips, block_count, block_rows, dec_heads, dec_size), 2, 0
    )
    everywhere = jnp.ones((clips, block_rows), dtype=bool)

    def scan_step(inner_state, key_block):
        return (
            fold_block(inner_state, dec_queries, key_block[0], key_block[1], everywhere, dec_scale),
            None,
        )

    result_state, _ = lax.scan(scan_step, start_state, grouped)
    fold_state = result_state
    dec_context = fold_state[2] / fold_state[1][..., None]
    dec_context = jnp.transpose(dec_context, (0, 2, 1, 3)).reshape(
        clips, own_rows // BLOCK, BLOCK, dec_width
    )
    return dec_context.astype(jnp.bfloat16)


def solution(mesh):
    in_specs = (
        P("seq", None),
        P(),
        P(),
        P(),
        P(),
        P(None, None, "head"),
        P("head", None),
        P(),
        P(),
        P(),
        P(),
        P(),
        P(),
        P(None, None, "head"),
    )
    out_specs = P(None, None, "seq", "head")
    return jax.shard_map(body, mesh=mesh, in_specs=in_specs, out_specs=out_specs, check_vma=False)
```

profile of v0, /device:TPU:1, one launch (start us, length us, event | category | flops | bytes accessed | tf_op | source)
XLA Modules:
  0.0 682.2 jit_solution(31880487049167066)
XLA Ops:
  14.1 3.8 collective-permute-start
  17.9 11.9 %collective-permute-done = bf16[1,2,384,352]{2,3,1,0:T(8,128)(2,1)} collective-permute-done((bf16[1,2,384,352]{2,3,1,0:T(8,128)(2,1)S(1)}, bf16[1,2,384,352]{2,3,1,0:T(8,128)(2,1)}, u32[]{:S(2)}, u32[]{:S(2)}) %collective-permute-start) | collective-permute-done | bytes 540704 | tf_op jit(solution)/shard_map/ppermute | solution.py:28
  33.3 23.1 %collective-permute-done.1 = bf16[2,2,384,352]{2,3,1,0:T(8,128)(2,1)} collective-permute-done((bf16[2,2,384,352]{2,3,1,0:T(8,128)(2,1)}, bf16[2,2,384,352]{2,3,1,0:T(8,128)(2,1)}, u32[]{:S(2)}, u32[]{:S(2)}) %collective-permute-start.1) | collective-permute-done | bytes 1081376 | tf_op jit(solution)/shard_map/ppermute | solution.py:28
  56.4 4.0 maximum_select_fusion.1
  68.0 40.4 %collective-permute-done.2 = bf16[4,2,384,352]{2,3,1,0:T(8,128)(2,1)} collective-permute-done((bf16[4,2,384,352]{2,3,1,0:T(8,128)(2,1)}, bf16[4,2,384,352]{2,3,1,0:T(8,128)(2,1)}, u32[]{:S(2)}, u32[]{:S(2)}) %collective-permute-start.2) | collective-permute-done | bytes 2162720 | tf_op jit(solution)/shard_map/ppermute | solution.py:28
  108.5 3.9 fusion.22
  116.3 4.2 reshape.477
  120.5 3.7 copy.37
  124.2 4.7 reshape.478
  128.9 11.2 %fusion.16 = (f32[4,384]{1,0:T(4,128)S(1)}, f32[4,384,3072]{2,1,0:T(8,128)}) fusion(pred[3072]{0:T(1024)(128)(4,1)S(1)} %lt.153, bf16[384,4,88]{0,2,1:T(8,128)(2,1)S(1)} %bitcast.138, bf16[3072,4,88]{0,2,1:T(8,128)(2,1)} %reshape.477), kind=kOutput, calls=%fused_computation.24 | convolution fusion | flops 844626432 | bytes 21316608 | tf_op jit(solution)/shard_map/cqhe,ckhe->chqk/dot_general | solution.py:48
  140.1 11.2 %fusion.17 = f32[4,384]{1,0:T(4,128)S(1)} fusion(f32[4,384,3072]{2,1,0:T(8,128)} %get-tuple-element.105, f32[4,384]{1,0:T(4,128)S(1)} %get-tuple-element.103, pred[3072]{0:T(1024)(128)(4,1)S(1)} %lt.153), kind=kLoop, calls=%fused_computation.25 | loop fusion | flops 23591424 | bytes 18889728 | tf_op jit(solution)/shard_map/reduce_sum | solution.py:54
  151.4 12.2 %fusion.62 = bf16[384,4,88]{0,2,1:T(8,128)(2,1)} fusion(bf16[3072,4,88]{0,2,1:T(8,128)(2,1)} %reshape.478, f32[4,384,3072]{2,1,0:T(8,128)} %get-tuple-element.105, f32[4,384]{1,0:T(4,128)S(1)} %get-tuple-element.103, pred[3072]{0:T(1024)(128)(4,1)S(1)} %lt.153, f32[384,4]{0,1:T(4,128)S(1)} %bitcast_add_fusion.1, f32[384,4]{0,1:T(4,128)S(1)} %get-tuple-element.102), kind=kOutput, calls=%fused_computation.86 | convolution fusion | flops 854470656 | bytes 21328896 | tf_op jit(solution)/shard_map/chqk,ckhe->chqe/dot_general | solution.py:56
  168.7 10.2 %all-to-all-start = ((s32[32,1,12]{2,1,0:T(1,128)}), s32[32,1,12]{2,1,0:T(1,128)S(1)}, u32[]{:S(2)}, u32[]{:S(2)}) async-start(s32[32,1,12]{2,1,0:T(1,128)} %bitcast.3), calls=%async_computation | async-start | bytes 32768 | tf_op jit(solution)/shard_map/all_to_all | solution.py:172
  179.9 36.2 %all-reduce.2.cloned.1.call-done = bf16[384,1408]{1,0:T(8,128)(2,1)} async-done(((bf16[384,1408]{1,0:T(8,128)(2,1)}), bf16[384,1408]{1,0:T(8,128)(2,1)}) %all-reduce.2.cloned.1.call-update) | async-done | bytes 1081360 | tf_op jit(solution)/shard_map/psum | solution.py:133
  221.6 9.3 %all-to-all-start.1 = ((bf16[32,12,512]{2,1,0:T(8,128)(2,1)}), bf16[32,12,512]{2,1,0:T(8,128)(2,1)S(1)}, u32[]{:S(2)}, u32[]{:S(2)}) async-start(bf16[32,12,512]{2,1,0:T(8,128)(2,1)} %reshape.479), calls=%async_computation.1 | async-start | bytes 1048576 | tf_op jit(solution)/shard_map/all_to_all | solution.py:171
  231.0 3.7 fusion.57
  236.2 6.3 all-to-all-done.1
  242.6 4.0 scatter_custom_fusion
  246.6 3.0 fusion.23
  257.6 108.6 %all-gather.2.cloned.1.call-done = bf16[2,4,16384,128]{3,2,1,0:T(8,128)(2,1)} async-done(((bf16[2,4,512,128]{3,2,1,0:T(8,128)(2,1)}), bf16[2,4,16384,128]{3,2,1,0:T(8,128)(2,1)}) %all-gather.2.cloned.1.call-update) | async-done | bytes 33554448 | tf_op jit(solution)/shard_map/all_gather | solution.py:215
  366.1 44.1 %copy.38 = bf16[2,4,16384,128]{2,3,1,0:T(8,128)(2,1)} copy(bf16[2,4,16384,128]{3,2,1,0:T(8,128)(2,1)} %all-gather.2.cloned.1.call-done) | data formatting | bytes 67108864 | tf_op jit(solution)/shard_map/all_gather | solution.py:215
  410.2 22.7 %copy.45 = bf16[128,8,32,512]{3,2,1,0:T(8,128)(2,1)} copy(bf16[128,8,32,512]{3,1,2,0:T(8,128)(2,1)} %bitcast.132) | data formatting | bytes 67108864
  432.9 22.9 %copy.40 = bf16[32,2,4,512,2,64]{3,5,4,2,1,0:T(8,128)(2,1)} copy(bf16[32,2,4,512,2,64]{3,0,5,4,2,1:T(8,128)(2,1)} %bitcast.133) | data formatting | bytes 67108864
  455.8 217.1 %while.15 = (s32[]{:T(128)}, f32[4,2,512]{2,1,0:T(2,128)S(1)}, f32[4,2,512]{2,1,0:T(2,128)S(1)}, f32[4,2,512,64]{2,3,1,0:T(8,128)S(1)}, bf16[32,2,4,512,2,64]{3,...) while((s32[]{:T(128)}, f32[4,2,512]{2,1,0:T(2,128)S(1)}, ...), condition=%wide.region_19.20_spmd.clone, body=%wide.region_16.19_spmd.clone.sunk | while | flops 554455040 | bytes 29098120 | solution.py:230
  (290 shorter events, 261.2 us)
Async XLA Ops:
  6.5 211.8 %copy-start = (bf16[1408,512]{1,0:T(8,128)(2,1)S(1)}, bf16[1408,512]{1,0:T(8,128)(2,1)}, u32[]{:S(2)}) copy-start(bf16[1408,512]{1,0:T(8,128)(2,1)} %param.25) | copy-start | bytes 4325380
  6.5 3.3 copy-start.4
  6.5 3.3 copy-start.12
  6.5 3.3 copy-start.13
  6.5 209.5 %all-reduce.2.cloned.1.call-start = ((), (), s32[]{:S(2)}) async-start(), calls=%async_computation.2 | async-start | bytes 2162688 | tf_op jit(solution)/shard_map/psum | solution.py:133
  14.1 15.7 %collective-permute-start = (bf16[1,2,384,352]{2,3,1,0:T(8,128)(2,1)S(1)}, bf16[1,2,384,352]{2,3,1,0:T(8,128)(2,1)}, u32[]{:S(2)}, u32[]{:S(2)}) collective-permute-start(bf16[1,2,384,352]{2,3,1,0:T(8,128)(2,1)S(1)} %maximum_bitcast_fusion), channel_id=1, source_target_pairs={{0,16},{16,0},{4,20},{20,4},{8,24},{24,8},{12,28},{28,12},{32,48},... | collective-permute-start | bytes 1622024 | tf_op jit(solution)/shard_map/ppermute | solution.py:28
  32.2 24.3 %collective-permute-start.1 = (bf16[2,2,384,352]{2,3,1,0:T(8,128)(2,1)}, bf16[2,2,384,352]{2,3,1,0:T(8,128)(2,1)}, u32[]{:S(2)}, u32[]{:S(2)}) collective-permute-start(bf16[2,2,384,352]{2,3,1,0:T(8,128)(2,1)} %maximum_select_fusion.2), channel_id=1, source_target_pairs={{0,32},{32,0},{4,36},{36,4},{8,40},{40,8},{12,44},{44,12},{16,48},... | collective-permute-start | bytes 3244040 | tf_op jit(solution)/shard_map/ppermute | solution.py:28
  33.3 31.1 %copy-start.11 = (s32[4,96]{1,0:T(4,128)S(1)}, s32[4,96]{1,0:T(4,128)}, u32[]{:S(2)}) copy-start(s32[4,96]{1,0:T(4,128)} %param.18) | copy-start | bytes 4612
  60.4 48.1 %collective-permute-start.2 = (bf16[4,2,384,352]{2,3,1,0:T(8,128)(2,1)}, bf16[4,2,384,352]{2,3,1,0:T(8,128)(2,1)}, u32[]{:S(2)}, u32[]{:S(2)}) collective-permute-start(bf16[4,2,384,352]{2,3,1,0:T(8,128)(2,1)} %maximum_select_fusion.1), channel_id=1, source_target_pairs={{0,64},{64,0},{4,68},{68,4},{8,72},{72,8},{12,76},{76,12},{16,80},... | collective-permute-start | bytes 6488072 | tf_op jit(solution)/shard_map/ppermute | solution.py:28
  151.4 12.2 %copy-start.6 = (bf16[352,1408]{1,0:T(8,128)(2,1)S(1)}, bf16[352,1408]{1,0:T(8,128)(2,1)}, u32[]{:S(2)}) copy-start(bf16[352,1408]{1,0:T(8,128)(2,1)} %param.22) | copy-start | bytes 2973700
  168.7 52.9 %all-to-all-start = ((s32[32,1,12]{2,1,0:T(1,128)}), s32[32,1,12]{2,1,0:T(1,128)S(1)}, u32[]{:S(2)}, u32[]{:S(2)}) async-start(s32[32,1,12]{2,1,0:T(1,128)} %bitcast.3), calls=%async_computation | async-start | bytes 32768 | tf_op jit(solution)/shard_map/all_to_all | solution.py:172
  179.8 38.5 %copy-start.14 = (f32[1408]{0:T(1024)S(1)}, f32[1408]{0:T(1024)}, u32[]{:S(2)}) copy-start(f32[1408]{0:T(1024)} %param.24) | copy-start | bytes 16900
  179.8 38.5 %copy-start.15 = (f32[1408]{0:T(1024)S(1)}, f32[1408]{0:T(1024)}, u32[]{:S(2)}) copy-start(f32[1408]{0:T(1024)} %param.23) | copy-start | bytes 16900
  216.1 1.7 copy-start.5
  221.6 20.9 %all-to-all-start.1 = ((bf16[32,12,512]{2,1,0:T(8,128)(2,1)}), bf16[32,12,512]{2,1,0:T(8,128)(2,1)S(1)}, u32[]{:S(2)}, u32[]{:S(2)}) async-start(bf16[32,12,512]{2,1,0:T(8,128)(2,1)} %reshape.479), calls=%async_computation.1 | async-start | bytes 1048576 | tf_op jit(solution)/shard_map/all_to_all | solution.py:171
  230.9 135.2 %all-gather.2.cloned.1.call-start = ((), (), s32[]{:S(2)}) async-start(), calls=%async_computation.3 | async-start | bytes 34603008 | tf_op jit(solution)/shard_map/all_gather | solution.py:215
  242.6 4.0 copy-start.8
  246.6 3.4 copy-start.2
  250.0 1.3 copy-start.9
  250.0 1.3 copy-start.10
  251.4 1.2 copy-start.7
  252.6 1.4 copy-start.3
  672.9 2.2 copy-start.1
Sparse Core Ops, SparseCore 0:
  166.5 49.5 all-reduce.1
  255.2 110.8 all-gather.1
where the time goes:
time: 693 us; the launch traced here: 682 us
  waiting for transfers between devices  227 us (33%)
  matrix products  207 us (30%)
  local copies, waits for them, and re-layouts  115 us (17%)
  other arithmetic  90.4 us (13%)
  starting transfers between devices  27.2 us (4%)
  between operations  14.1 us (2%)
    all_gather x1, waiting for transfers between devices, body(): shard_part = lax.all_gather(stacked, 'seq', axis=2, tiled=True)  109 us
    dot_general x33, matrix products, fold_block(): jnp.einsum('chqk,ckhe->chqe', weights, value_rows, preferred_element_type...  105 us
    dot_general x33, matrix products, fold_block(): jnp.einsum('cqhe,ckhe->chqk', queries, key_rows, preferred_element_type=j...  86.7 us
    ppermute x3, waiting for transfers between devices, from_partner(): return lax.ppermute(block, axis, route)  75.4 us
    reduce_sum x33, other arithmetic, fold_block(): running_sum = running_sum * factor + jnp.sum(raised, axis=-1)  56.9 us
    unnamed x35, local copies, waits for them, and re-layouts  46.1 us
    all_gather x1, local copies, waits for them, and re-layouts, body(): shard_part = lax.all_gather(stacked, 'seq', axis=2, tiled=True)  44.1 us
    psum x1, waiting for transfers between devices, body(): lax.psum(partial_out.astype(jnp.bfloat16), 'head').astype(jnp.float32)  36.2 us
  transfers between devices with their start and end apart: 7, of which 6 were waited for; matrix products, arithmetic and copies ran while one was open for 3% of the time, Pallas kernels for 0%

commit v1 on v0

--- a/solution.py
+++ b/solution.py
@@ -212,7 +212,8 @@
         "crd,de->cre", dec_normed, dec_qkv[2], preferred_element_type=jnp.float32
     ).astype(jnp.bfloat16)
     stacked = jnp.stack([dec_key, dec_value])
-    shard_part = lax.all_gather(stacked, "seq", axis=2, tiled=True)
+    frame_out = jax.lax.all_gather(stacked, "seq")
+    shard_part = jnp.concatenate(frame_out, 2)
     row_count = shard_part.shape[2]
     block_count = row_count // own_rows
     block_rows = row_count // block_count

time: 693 us -> 648 us (0.935)
  local copies, waits for them, and re-layouts: 115 us -> 69.7 us
    unnamed x35 -> x33, local copies, waits for them, and re-layouts: 46.1 us -> 0.49 us
    reshape x0 -> x1, local copies, waits for them, and re-layouts: none -> 44.2 us  [body(): shard_part = jnp.concatenate(frame_out, 2)]
    all_gather x1 -> x0, local copies, waits for them, and re-layouts: 44.1 us -> none  [body(): shard_part = lax.all_gather(stacked, 'seq', axis=2, tiled=True)]
where the time goes in v1:
time: 648 us; the launch traced here: 637 us
  waiting for transfers between devices  227 us (35%)
  matrix products  207 us (32%)
  other arithmetic  90.4 us (14%)
  local copies, waits for them, and re-layouts  69.7 us (11%)
  starting transfers between devices  27.2 us (4%)
  between operations  14.1 us (2%)
    all_gather x1, waiting for transfers between devices, body(): frame_out = jax.lax.all_gather(stacked, 'seq')  109 us
    dot_general x33, matrix products, fold_block(): jnp.einsum('chqk,ckhe->chqe', weights, value_rows, preferred_element_type...  105 us
    dot_general x33, matrix products, fold_block(): jnp.einsum('cqhe,ckhe->chqk', queries, key_rows, preferred_element_type=j...  86.7 us
    ppermute x3, waiting for transfers between devices, from_partner(): return lax.ppermute(block, axis, route)  75.4 us
    reduce_sum x33, other arithmetic, fold_block(): running_sum = running_sum * factor + jnp.sum(raised, axis=-1)  56.9 us
    reshape x1, local copies, waits for them, and re-layouts, body(): shard_part = jnp.concatenate(frame_out, 2)  44.2 us
    psum x1, waiting for transfers between devices, body(): lax.psum(partial_out.astype(jnp.bfloat16), 'head').astype(jnp.float32)  36.2 us
  transfers between devices with their start and end apart: 7, of which 6 were waited for; matrix products, arithmetic and copies ran while one was open for 3% of the time, Pallas kernels for 0%

profile of v1, /device:TPU:1, one launch (start us, length us, event | category | flops | bytes accessed | tf_op | source)
XLA Modules:
  0.0 636.7 jit_solution(3507368074697231272)
XLA Ops:
  14.1 3.8 collective-permute-start
  17.9 11.9 %collective-permute-done = bf16[1,2,384,352]{2,3,1,0:T(8,128)(2,1)} collective-permute-done((bf16[1,2,384,352]{2,3,1,0:T(8,128)(2,1)S(1)}, bf16[1,2,384,352]{2,3,1,0:T(8,128)(2,1)}, u32[]{:S(2)}, u32[]{:S(2)}) %collective-permute-start) | collective-permute-done | bytes 540704 | tf_op jit(solution)/shard_map/ppermute | solution.py:28
  33.3 23.1 %collective-permute-done.1 = bf16[2,2,384,352]{2,3,1,0:T(8,128)(2,1)} collective-permute-done((bf16[2,2,384,352]{2,3,1,0:T(8,128)(2,1)}, bf16[2,2,384,352]{2,3,1,0:T(8,128)(2,1)}, u32[]{:S(2)}, u32[]{:S(2)}) %collective-permute-start.1) | collective-permute-done | bytes 1081376 | tf_op jit(solution)/shard_map/ppermute | solution.py:28
  56.4 4.0 maximum_select_fusion.1
  68.0 40.4 %collective-permute-done.2 = bf16[4,2,384,352]{2,3,1,0:T(8,128)(2,1)} collective-permute-done((bf16[4,2,384,352]{2,3,1,0:T(8,128)(2,1)}, bf16[4,2,384,352]{2,3,1,0:T(8,128)(2,1)}, u32[]{:S(2)}, u32[]{:S(2)}) %collective-permute-start.2) | collective-permute-done | bytes 2162720 | tf_op jit(solution)/shard_map/ppermute | solution.py:28
  108.5 3.9 fusion.22
  116.3 4.2 reshape.477
  120.5 3.7 copy.35
  124.2 4.7 reshape.478
  128.9 11.2 %fusion.16 = (f32[4,384]{1,0:T(4,128)S(1)}, f32[4,384,3072]{2,1,0:T(8,128)}) fusion(pred[3072]{0:T(1024)(128)(4,1)S(1)} %lt.153, bf16[384,4,88]{0,2,1:T(8,128)(2,1)S(1)} %bitcast.135, bf16[3072,4,88]{0,2,1:T(8,128)(2,1)} %reshape.477), kind=kOutput, calls=%fused_computation.24 | convolution fusion | flops 844626432 | bytes 21316608 | tf_op jit(solution)/shard_map/cqhe,ckhe->chqk/dot_general | solution.py:48
  140.1 11.2 %fusion.17 = f32[4,384]{1,0:T(4,128)S(1)} fusion(f32[4,384,3072]{2,1,0:T(8,128)} %get-tuple-element.87, f32[4,384]{1,0:T(4,128)S(1)} %get-tuple-element.85, pred[3072]{0:T(1024)(128)(4,1)S(1)} %lt.153), kind=kLoop, calls=%fused_computation.25 | loop fusion | flops 23591424 | bytes 18889728 | tf_op jit(solution)/shard_map/reduce_sum | solution.py:54
  151.4 12.2 %fusion.62 = bf16[384,4,88]{0,2,1:T(8,128)(2,1)} fusion(bf16[3072,4,88]{0,2,1:T(8,128)(2,1)} %reshape.478, f32[4,384,3072]{2,1,0:T(8,128)} %get-tuple-element.87, f32[4,384]{1,0:T(4,128)S(1)} %get-tuple-element.85, pred[3072]{0:T(1024)(128)(4,1)S(1)} %lt.153, f32[384,4]{0,1:T(4,128)S(1)} %bitcast_add_fusion.1, f32[384,4]{0,1:T(4,128)S(1)} %get-tuple-element.84), kind=kOutput, calls=%fused_computation.86 | convolution fusion | flops 854470656 | bytes 21328896 | tf_op jit(solution)/shard_map/chqk,ckhe->chqe/dot_general | solution.py:56
  168.7 10.2 %all-to-all-start = ((s32[32,1,12]{2,1,0:T(1,128)}), s32[32,1,12]{2,1,0:T(1,128)S(1)}, u32[]{:S(2)}, u32[]{:S(2)}) async-start(s32[32,1,12]{2,1,0:T(1,128)} %bitcast.3), calls=%async_computation | async-start | bytes 32768 | tf_op jit(solution)/shard_map/all_to_all | solution.py:172
  179.9 36.2 %all-reduce.2.cloned.1.call-done = bf16[384,1408]{1,0:T(8,128)(2,1)} async-done(((bf16[384,1408]{1,0:T(8,128)(2,1)}), bf16[384,1408]{1,0:T(8,128)(2,1)}) %all-reduce.2.cloned.1.call-update) | async-done | bytes 1081360 | tf_op jit(solution)/shard_map/psum | solution.py:133
  221.6 9.3 %all-to-all-start.1 = ((bf16[32,12,512]{2,1,0:T(8,128)(2,1)}), bf16[32,12,512]{2,1,0:T(8,128)(2,1)S(1)}, u32[]{:S(2)}, u32[]{:S(2)}) async-start(bf16[32,12,512]{2,1,0:T(8,128)(2,1)} %reshape.479), calls=%async_computation.1 | async-start | bytes 1048576 | tf_op jit(solution)/shard_map/all_to_all | solution.py:171
  231.0 3.7 fusion.57
  236.2 6.3 all-to-all-done.1
  242.6 4.0 scatter_custom_fusion
  246.6 3.0 fusion.23
  257.6 108.6 %all-gather.3.cloned.1.call-done = bf16[64,4,512,128]{3,2,1,0:T(8,128)(2,1)} async-done(((bf16[2,4,512,128]{3,2,1,0:T(8,128)(2,1)}), bf16[64,4,512,128]{3,2,1,0:T(8,128)(2,1)}) %all-gather.3.cloned.1.call-update) | async-done | bytes 33554448 | tf_op jit(solution)/shard_map/all_gather | solution.py:215
  366.1 44.2 %copy.36 = bf16[2,4,32,512,128]{3,4,1,0,2:T(8,128)(2,1)} copy(bf16[2,4,32,512,128]{4,3,1,0,2:T(8,128)(2,1)} %bitcast.130) | data formatting | bytes 67108864 | tf_op jit(solution)/shard_map/reshape | solution.py:216
  410.3 217.1 %while.15 = (s32[]{:T(128)}, f32[4,2,512]{2,1,0:T(2,128)S(1)}, f32[4,2,512]{2,1,0:T(2,128)S(1)}, f32[4,2,512,64]{2,3,1,0:T(8,128)S(1)}, bf16[32,2,4,512,2,64]{3,...) while((s32[]{:T(128)}, f32[4,2,512]{2,1,0:T(2,128)S(1)}, ...), condition=%wide.region_19.20_spmd.clone, body=%wide.region_16.19_spmd.clone.sunk | while | flops 554455040 | bytes 29098120 | solution.py:231
  427.7 2.9 fusion.145
  543.1 2.9 fusion.145
  (288 shorter events, 255.4 us)
Async XLA Ops:
  6.5 211.8 %copy-start = (bf16[1408,512]{1,0:T(8,128)(2,1)S(1)}, bf16[1408,512]{1,0:T(8,128)(2,1)}, u32[]{:S(2)}) copy-start(bf16[1408,512]{1,0:T(8,128)(2,1)} %param.25) | copy-start | bytes 4325380
  6.5 3.3 copy-start.4
  6.5 3.3 copy-start.12
  6.5 3.3 copy-start.13
  6.5 209.5 %all-reduce.2.cloned.1.call-start = ((), (), s32[]{:S(2)}) async-start(), calls=%async_computation.2 | async-start | bytes 2162688 | tf_op jit(solution)/shard_map/psum | solution.py:133
  14.1 15.7 %collective-permute-start = (bf16[1,2,384,352]{2,3,1,0:T(8,128)(2,1)S(1)}, bf16[1,2,384,352]{2,3,1,0:T(8,128)(2,1)}, u32[]{:S(2)}, u32[]{:S(2)}) collective-permute-start(bf16[1,2,384,352]{2,3,1,0:T(8,128)(2,1)S(1)} %maximum_bitcast_fusion), channel_id=1, source_target_pairs={{0,16},{16,0},{4,20},{20,4},{8,24},{24,8},{12,28},{28,12},{32,48},... | collective-permute-start | bytes 1622024 | tf_op jit(solution)/shard_map/ppermute | solution.py:28
  32.2 24.3 %collective-permute-start.1 = (bf16[2,2,384,352]{2,3,1,0:T(8,128)(2,1)}, bf16[2,2,384,352]{2,3,1,0:T(8,128)(2,1)}, u32[]{:S(2)}, u32[]{:S(2)}) collective-permute-start(bf16[2,2,384,352]{2,3,1,0:T(8,128)(2,1)} %maximum_select_fusion.2), channel_id=1, source_target_pairs={{0,32},{32,0},{4,36},{36,4},{8,40},{40,8},{12,44},{44,12},{16,48},... | collective-permute-start | bytes 3244040 | tf_op jit(solution)/shard_map/ppermute | solution.py:28
  33.3 31.1 %copy-start.11 = (s32[4,96]{1,0:T(4,128)S(1)}, s32[4,96]{1,0:T(4,128)}, u32[]{:S(2)}) copy-start(s32[4,96]{1,0:T(4,128)} %param.18) | copy-start | bytes 4612
  60.4 48.1 %collective-permute-start.2 = (bf16[4,2,384,352]{2,3,1,0:T(8,128)(2,1)}, bf16[4,2,384,352]{2,3,1,0:T(8,128)(2,1)}, u32[]{:S(2)}, u32[]{:S(2)}) collective-permute-start(bf16[4,2,384,352]{2,3,1,0:T(8,128)(2,1)} %maximum_select_fusion.1), channel_id=1, source_target_pairs={{0,64},{64,0},{4,68},{68,4},{8,72},{72,8},{12,76},{76,12},{16,80},... | collective-permute-start | bytes 6488072 | tf_op jit(solution)/shard_map/ppermute | solution.py:28
  151.4 12.2 %copy-start.6 = (bf16[352,1408]{1,0:T(8,128)(2,1)S(1)}, bf16[352,1408]{1,0:T(8,128)(2,1)}, u32[]{:S(2)}) copy-start(bf16[352,1408]{1,0:T(8,128)(2,1)} %param.22) | copy-start | bytes 2973700
  168.7 52.9 %all-to-all-start = ((s32[32,1,12]{2,1,0:T(1,128)}), s32[32,1,12]{2,1,0:T(1,128)S(1)}, u32[]{:S(2)}, u32[]{:S(2)}) async-start(s32[32,1,12]{2,1,0:T(1,128)} %bitcast.3), calls=%async_computation | async-start | bytes 32768 | tf_op jit(solution)/shard_map/all_to_all | solution.py:172
  179.8 38.5 %copy-start.14 = (f32[1408]{0:T(1024)S(1)}, f32[1408]{0:T(1024)}, u32[]{:S(2)}) copy-start(f32[1408]{0:T(1024)} %param.24) | copy-start | bytes 16900
  179.8 38.5 %copy-start.15 = (f32[1408]{0:T(1024)S(1)}, f32[1408]{0:T(1024)}, u32[]{:S(2)}) copy-start(f32[1408]{0:T(1024)} %param.23) | copy-start | bytes 16900
  216.1 1.7 copy-start.5
  221.6 20.9 %all-to-all-start.1 = ((bf16[32,12,512]{2,1,0:T(8,128)(2,1)}), bf16[32,12,512]{2,1,0:T(8,128)(2,1)S(1)}, u32[]{:S(2)}, u32[]{:S(2)}) async-start(bf16[32,12,512]{2,1,0:T(8,128)(2,1)} %reshape.479), calls=%async_computation.1 | async-start | bytes 1048576 | tf_op jit(solution)/shard_map/all_to_all | solution.py:171
  230.9 135.2 %all-gather.3.cloned.1.call-start = ((), (), s32[]{:S(2)}) async-start(), calls=%async_computation.3 | async-start | bytes 34603008 | tf_op jit(solution)/shard_map/all_gather | solution.py:215
  242.6 4.0 copy-start.8
  246.6 3.4 copy-start.2
  250.0 1.3 copy-start.9
  250.0 1.3 copy-start.10
  251.4 1.2 copy-start.7
  252.6 1.4 copy-start.3
  627.4 2.2 copy-start.1
Sparse Core Ops, SparseCore 0:
  166.5 49.5 all-reduce.1
  255.2 110.8 all-gather.2
